TPU v7x, 32 devices: a whole 2x2x4 slice. The times are simulated.
32 devices in a mesh: fsdp: 16 (over z, y, core), sp: 2 (over x).
Axes of the slice: x: 2, y: 2, z: 4, core: 2. Of those that a mesh axis runs over, the one named last changes fastest.
Arguments:
- latents: bfloat16 [32, 256, 768], P('fsdp', 'sp'), may hold values from -6 to 6
- condition: bfloat16 [32, 768], P('fsdp'), may hold values from -6 to 6
- cotangent: bfloat16 [32, 256, 768], P('fsdp', 'sp'), may hold values from -6 to 6
- w_ada: bfloat16 [768, 4608], P('fsdp'), may hold values from -0.21875 to 0.21875
- b_ada: bfloat16 [4608], P('fsdp'), may hold values from -3 to 3
- w_qkv: bfloat16 [768, 2304], P('fsdp'), may hold values from -0.21875 to 0.21875
- b_query: bfloat16 [768], P('fsdp'), may hold values from -3 to 3
- b_value: bfloat16 [768], P('fsdp'), may hold values from -3 to 3
- w_out: bfloat16 [768, 768], P('fsdp'), may hold values from -0.875 to 0.875
- b_out: bfloat16 [768], P('fsdp'), may hold values from -3 to 3
- w_up: bfloat16 [768, 3072], P('fsdp'), may hold values from -0.21875 to 0.21875
- b_up: bfloat16 [3072], P('fsdp'), may hold values from -3 to 3
- w_down: bfloat16 [3072, 768], P('fsdp'), may hold values from -0.109375 to 0.109375
- b_down: bfloat16 [768], P('fsdp'), may hold values from -3 to 3
Outputs:
- output: bfloat16 [32, 256, 768], P('fsdp', 'sp')
- grad_latents: float32 [32, 256, 768], P('fsdp', 'sp')
- grad_condition: float32 [32, 768], P('fsdp')
- grad_w_ada: float32 [768, 4608], P(('fsdp', 'sp'))
- grad_b_ada: float32 [4608], P(('fsdp', 'sp'))
- grad_w_qkv: float32 [768, 2304], P(('fsdp', 'sp'))
- grad_b_query: float32 [768], P(('fsdp', 'sp'))
- grad_b_value: float32 [768], P(('fsdp', 'sp'))
- grad_w_out: float32 [768, 768], P(('fsdp', 'sp'))
- grad_b_out: float32 [768], P(('fsdp', 'sp'))
- grad_w_up: float32 [768, 3072], P(('fsdp', 'sp'))
- grad_b_up: float32 [3072], P(('fsdp', 'sp'))
- grad_w_down: float32 [3072, 768], P(('fsdp', 'sp'))
- grad_b_down: float32 [768], P(('fsdp', 'sp'))
All inputs are finite; a program needn't handle non-finite values.
Results may differ from a plain program's by a relative error of at most 0.015.
The roundings to bfloat16 on the way count: a program that leaves them out, or rounds other values in their place, can miss the bound.
Values may be sent and summed in bfloat16 or wider, within the bound.
A program may use at most 256 MiB of HBM per device.

v0:
```python
import jax
import jax.numpy as jnp
from jax import lax
from jax.sharding import PartitionSpec as P

D = 768
H = 12
HD = 64
eps = 1e-06


def normalize(values):
    centered = values - jnp.mean(values, axis=-1, keepdims=True)
    inverse = lax.rsqrt(jnp.mean(centered * centered, axis=-1, keepdims=True) + eps)
    return (centered * inverse, inverse)


def norm_back(grad_in, normed, inverse):
    return inverse * (
        grad_in
        - jnp.mean(grad_in, axis=-1, keepdims=True)
        - normed * jnp.mean(grad_in * normed, axis=-1, keepdims=True)
    )


def gelu_tanh(values):
    return jax.nn.gelu(values, approximate=True)


def silu_back(values, grad_out):
    return jax.vjp(jax.nn.silu, values)[1](grad_out)[0]


def gelu_back(values, grad_out):
    return jax.vjp(gelu_tanh, values)[1](grad_out)[0]


LANES = 2048


def reduce_rows(grad):
    return lax.psum_scatter(
        grad.astype(jnp.bfloat16), ("fsdp", "sp"), scatter_dimension=0, tiled=True
    ).astype(jnp.float32)


def body(
    latents,
    condition,
    cotangent,
    w_ada,
    b_ada,
    w_qkv,
    b_query,
    b_value,
    w_out,
    b_out,
    w_up,
    b_up,
    w_down,
    b_down,
):
    f32 = jnp.float32
    bf16 = jnp.bfloat16
    fsdp_count = lax.axis_size("fsdp")
    sp_count = lax.axis_size("sp")
    owners = fsdp_count * sp_count
    fsdp_index = lax.axis_index("fsdp")
    sp_index = lax.axis_index("sp")
    owner_index = fsdp_index * sp_count + sp_index
    pair_latents = latents.shape[0]
    own_latents = pair_latents // sp_count
    latent_total = pair_latents * fsdp_count
    tokens_all = latents.shape[1] * sp_count
    scale_factor = HD ** (-0.5)
    small = [condition.reshape(-1), b_ada, b_query, b_value, b_out, b_up, b_down]
    width = sum((part.size for part in small))
    padded = -(-width // LANES) * LANES
    small.append(jnp.zeros((padded - width,), bf16))
    small_all = lax.all_gather(
        jnp.concatenate(small).reshape(1, padded // 128, 128), "fsdp", axis=0, tiled=True
    ).reshape(fsdp_count, padded)
    pieces = []
    start = 0
    for part in small[:-1]:
        pieces.append(small_all[:, start : start + part.size].reshape(-1))
        start = start + part.size
    cond_all, ada_bias, query_bias, value_bias, out_bias, up_bias, down_bias = pieces
    cond_all = cond_all.reshape(latent_total, D).astype(f32)
    silu_all = jax.nn.silu(cond_all)
    inputs = lax.all_to_all(latents, "sp", split_axis=0, concat_axis=1, tiled=True).astype(f32)
    grad_out = lax.all_to_all(cotangent, "sp", split_axis=0, concat_axis=1, tiled=True).astype(f32)
    ada_rows = w_ada.shape[0]
    silu_mine = lax.dynamic_index_in_dim(
        silu_all.astype(bf16).reshape(fsdp_count, sp_count, own_latents, D), sp_index, 1, False
    )
    silu_mine = lax.dynamic_index_in_dim(
        silu_mine.reshape(fsdp_count * own_latents, fsdp_count, ada_rows), fsdp_index, 1, False
    )
    mod_part = jnp.dot(silu_mine, w_ada, preferred_element_type=f32)
    mod_part = lax.all_to_all(
        mod_part.reshape(fsdp_count, own_latents * 6 * D),
        "fsdp",
        split_axis=0,
        concat_axis=0,
        tiled=True,
    )
    modulate = jnp.sum(mod_part, axis=0).reshape(own_latents, 6 * D) + ada_bias.astype(f32)
    mod_parts = modulate.reshape(own_latents, 6, 1, D)
    shift_one, scale_one, gate_one = (mod_parts[:, 0], mod_parts[:, 1], mod_parts[:, 2])
    shift_two, scale_two, gate_two = (mod_parts[:, 3], mod_parts[:, 4], mod_parts[:, 5])
    qkv_full = lax.all_gather(w_qkv, "fsdp", axis=0, tiled=True)
    out_full = lax.all_gather(w_out, "fsdp", axis=0, tiled=True)
    up_full = lax.all_gather(w_up, "fsdp", axis=0, tiled=True)
    down_full = lax.all_gather(w_down, "fsdp", axis=0, tiled=True)
    normed_one, inverse_one = normalize(inputs)
    attn_in = (normed_one * (1.0 + scale_one) + shift_one).astype(bf16)
    qkv_bias = jnp.concatenate([query_bias, jnp.zeros_like(query_bias), value_bias]).astype(f32)
    projected = (
        jnp.einsum("btd,de->bte", attn_in, qkv_full, preferred_element_type=f32) + qkv_bias
    ).astype(bf16)
    heads = projected.reshape(own_latents, tokens_all, 3, H, HD).transpose(2, 0, 3, 1, 4)
    queries, key_heads, value_heads = (heads[0], heads[1], heads[2])
    scores = (
        jnp.einsum("bhqd,bhkd->bhqk", queries, key_heads, preferred_element_type=f32) * scale_factor
    )
    log_total = jnp.log(jnp.sum(jnp.exp(scores), axis=-1, keepdims=True))
    soft_float = jnp.exp(scores - log_total)
    soft_half = soft_float.astype(bf16)
    mixed = jnp.einsum(
        "bhqk,bhkd->bhqd", soft_half, value_heads, preferred_element_type=f32
    ).astype(bf16)
    mixed_tokens = mixed.transpose(0, 2, 1, 3).reshape(own_latents, tokens_all, D)
    attn_proj = jnp.einsum(
        "btd,de->bte", mixed_tokens, out_full, preferred_element_type=f32
    ) + out_bias.astype(f32)
    residual = inputs + gate_one * attn_proj
    normed_two, inverse_two = normalize(residual)
    mlp_in = (normed_two * (1.0 + scale_two) + shift_two).astype(bf16)
    up_value = jnp.einsum(
        "btd,df->btf", mlp_in, up_full, preferred_element_type=f32
    ) + up_bias.astype(f32)
    activated = gelu_tanh(up_value).astype(bf16)
    down_value = jnp.einsum(
        "btf,fd->btd", activated, down_full, preferred_element_type=f32
    ) + down_bias.astype(f32)
    output = (residual + gate_two * down_value).astype(bf16)
    output = lax.all_to_all(output, "sp", split_axis=1, concat_axis=0, tiled=True)
    grad_gate_two = jnp.sum(grad_out * down_value, axis=1)
    grad_down = (grad_out * gate_two).astype(bf16)
    gw_down = jnp.einsum("btf,btd->fd", activated, grad_down, preferred_element_type=f32)
    own_down = reduce_rows(gw_down)
    gb_down = jnp.sum(grad_down.astype(f32), axis=(0, 1))
    grad_act = jnp.einsum("btd,fd->btf", grad_down, down_full, preferred_element_type=f32)
    grad_up = gelu_back(up_value, grad_act).astype(bf16)
    gw_up = jnp.einsum("btd,btf->df", mlp_in, grad_up, preferred_element_type=f32)
    own_up = reduce_rows(gw_up)
    gb_up = jnp.sum(grad_up.astype(f32), axis=(0, 1))
    grad_mlp = jnp.einsum("btf,df->btd", grad_up, up_full, preferred_element_type=f32)
    grad_scale_two = jnp.sum(grad_mlp * normed_two, axis=1)
    grad_shift_two = jnp.sum(grad_mlp, axis=1)
    grad_resid = grad_out + norm_back(grad_mlp * (1.0 + scale_two), normed_two, inverse_two)
    grad_gate_one = jnp.sum(grad_resid * attn_proj, axis=1)
    grad_proj = (grad_resid * gate_one).astype(bf16)
    gw_out = jnp.einsum("btd,bte->de", mixed_tokens, grad_proj, preferred_element_type=f32)
    own_out = reduce_rows(gw_out)
    gb_out = jnp.sum(grad_proj.astype(f32), axis=(0, 1))
    grad_mixed = jnp.einsum("bte,de->btd", grad_proj, out_full, preferred_element_type=f32).astype(
        bf16
    )
    grad_heads = grad_mixed.reshape(own_latents, tokens_all, H, HD).transpose(0, 2, 1, 3)
    grad_soft = jnp.einsum("bhqd,bhkd->bhqk", grad_heads, value_heads, preferred_element_type=f32)
    delta_sum = jnp.sum(soft_float * grad_soft, axis=-1, keepdims=True)
    grad_scores = (soft_float * (grad_soft - delta_sum)).astype(bf16)
    grad_queries = (
        jnp.einsum("bhqk,bhkd->bhqd", grad_scores, key_heads, preferred_element_type=f32)
        * scale_factor
    ).astype(bf16)
    grad_keys = (
        jnp.einsum("bhqk,bhqd->bhkd", grad_scores, queries, preferred_element_type=f32)
        * scale_factor
    ).astype(bf16)
    grad_values = jnp.einsum(
        "bhqk,bhqd->bhkd", soft_half, grad_heads, preferred_element_type=f32
    ).astype(bf16)
    grad_tokens = (
        jnp.stack([grad_queries, grad_keys, grad_values], axis=0)
        .transpose(1, 3, 0, 2, 4)
        .reshape(own_latents, tokens_all, 3 * D)
    )
    gw_qkv = jnp.einsum("btd,bte->de", attn_in, grad_tokens, preferred_element_type=f32)
    own_qkv = reduce_rows(gw_qkv)
    grad_tok_float = grad_tokens.astype(f32)
    gb_query = jnp.sum(grad_tok_float[:, :, :D], axis=(0, 1))
    gb_value = jnp.sum(grad_tok_float[:, :, 2 * D :], axis=(0, 1))
    grad_attn_in = jnp.einsum("bte,de->btd", grad_tokens, qkv_full, preferred_element_type=f32)
    grad_scale_one = jnp.sum(grad_attn_in * normed_one, axis=1)
    grad_shift_one = jnp.sum(grad_attn_in, axis=1)
    grad_latents = grad_resid + norm_back(grad_attn_in * (1.0 + scale_one), normed_one, inverse_one)
    grad_latents = lax.all_to_all(grad_latents, "sp", split_axis=1, concat_axis=0, tiled=True)
    grad_small = [
        grad_shift_one.reshape(-1),
        grad_scale_one.reshape(-1),
        grad_gate_one.reshape(-1),
        grad_shift_two.reshape(-1),
        grad_scale_two.reshape(-1),
        grad_gate_two.reshape(-1),
        gb_query,
        gb_value,
        gb_out,
        gb_up,
        gb_down,
    ]
    grad_small_all = lax.all_gather(jnp.concatenate(grad_small), ("fsdp", "sp"), axis=0)
    mod_width = 6 * own_latents * D
    grad_mod = (
        grad_small_all[:, :mod_width]
        .reshape(owners, 6, own_latents, D)
        .transpose(0, 2, 1, 3)
        .reshape(latent_total, 6 * D)
    )
    bias_sums = jnp.sum(grad_small_all[:, mod_width:], axis=0)
    own_bias = []
    start = 0
    for part in grad_small[6:]:
        piece = bias_sums[start : start + part.size].reshape(owners, -1)
        own_bias.append(lax.dynamic_index_in_dim(piece, owner_index, 0, False))
        start = start + part.size
    own_gb_query, own_gb_value, own_gb_out, own_gb_up, own_gb_down = own_bias
    silu_rows = lax.dynamic_index_in_dim(
        silu_all.reshape(latent_total, owners, D // owners), owner_index, 1, False
    )
    own_ada = jnp.dot(silu_rows.T, grad_mod, precision=lax.Precision.HIGHEST)
    own_gb_ada = lax.dynamic_index_in_dim(
        jnp.sum(grad_mod, axis=0).reshape(owners, -1), owner_index, 0, False
    )
    grad_silu = jnp.dot(grad_mod.astype(bf16), w_ada.T, preferred_element_type=f32)
    grad_silu = lax.all_to_all(
        grad_silu.reshape(fsdp_count, pair_latents * ada_rows),
        "fsdp",
        split_axis=0,
        concat_axis=0,
        tiled=True,
    )
    grad_silu = (
        grad_silu.reshape(fsdp_count, pair_latents, ada_rows)
        .transpose(1, 0, 2)
        .reshape(pair_latents, D)
    )
    grad_condition = silu_back(condition.astype(f32), grad_silu)
    return (
        output,
        grad_latents,
        grad_condition,
        own_ada,
        own_gb_ada,
        own_qkv,
        own_gb_query,
        own_gb_value,
        own_out,
        own_gb_out,
        own_up,
        own_gb_up,
        own_down,
        own_gb_down,
    )


def solution(mesh):
    in_specs = (
        P("fsdp", "sp", None),
        P("fsdp", None),
        P("fsdp", "sp", None),
        P("fsdp", None),
        P("fsdp"),
        P("fsdp", None),
        P("fsdp"),
        P("fsdp"),
        P("fsdp", None),
        P("fsdp"),
        P("fsdp", None),
        P("fsdp"),
        P("fsdp", None),
        P("fsdp"),
    )
    out_specs = (
        P("fsdp", "sp", None),
        P("fsdp", "sp", None),
        P("fsdp", None),
        P(("fsdp", "sp"), None),
        P(("fsdp", "sp")),
        P(("fsdp", "sp"), None),
        P(("fsdp", "sp")),
        P(("fsdp", "sp")),
        P(("fsdp", "sp"), None),
        P(("fsdp", "sp")),
        P(("fsdp", "sp"), None),
        P(("fsdp", "sp")),
        P(("fsdp", "sp"), None),
        P(("fsdp", "sp")),
    )
    return jax.shard_map(body, mesh=mesh, in_specs=in_specs, out_specs=out_specs, check_vma=False)
```

profile of v0, /device:TPU:0, one launch (start us, length us, event | category | flops | bytes accessed | tf_op | source)
XLA Modules:
  0.0 743.5 jit_solution(2040132775007080298)
XLA Ops:
  10.0 4.2 all-to-all-start
  14.9 4.1 concatenate.17
  19.1 22.7 %all_gather.21 = bf16[16,32,128]{2,1,0:T(8,128)(2,1)S(1)} all-gather(bf16[1,32,128]{2,1,0:T(8,128)(2,1)S(1)} %bitcast.185), channel_id=1, replica_groups=mesh['fsdp'=16,'sp'=2] {'fsdp'}, dimensions={0}, use_global_device_ids=true | all-gather | bytes 139264 | tf_op jit(solution)/shard_map/all_gather | solution.py:80
  48.0 13.6 %all-to-all-done.1 = f32[16,1,4608]{2,1,0:T(1,128)S(1)} async-done(((f32[16,1,4608]{2,1,0:T(1,128)}), f32[16,1,4608]{2,1,0:T(1,128)S(1)}, u32[]{:S(2)}, u32[]{:S(2)}) %all-to-all-start.1) | async-done | bytes 294944 | tf_op jit(solution)/shard_map/all_to_all | solution.py:101
  61.7 3.8 all-to-all-start.3
  65.8 6.4 all-to-all-done.3
  73.4 4.2 fusion.1
  81.4 4.8 convolution_convert_fusion.4
  86.2 18.5 %all-gather.10.cloned.1.call-done = bf16[768,768]{1,0:T(8,128)(2,1)} async-done(((bf16[48,768]{1,0:T(8,128)(2,1)}), bf16[768,768]{1,0:T(8,128)(2,1)}) %all-gather.10.cloned.1.call-update) | async-done | bytes 1179664 | tf_op jit(solution)/shard_map/all_gather | solution.py:113
  107.7 51.3 %all-gather.14.cloned.1.call-done = bf16[3072,768]{1,0:T(8,128)(2,1)} async-done(((bf16[192,768]{1,0:T(8,128)(2,1)}), bf16[3072,768]{1,0:T(8,128)(2,1)}) %all-gather.14.cloned.1.call-update) | async-done | bytes 4718608 | tf_op jit(solution)/shard_map/all_gather | solution.py:115
  159.0 5.5 fusion.83
  164.5 48.3 %all-gather.12.cloned.1.call-done = bf16[768,3072]{1,0:T(8,128)(2,1)} async-done(((bf16[48,3072]{1,0:T(8,128)(2,1)}), bf16[768,3072]{1,0:T(8,128)(2,1)}) %all-gather.12.cloned.1.call-update) | async-done | bytes 4718608 | tf_op jit(solution)/shard_map/all_gather | solution.py:114
  212.8 7.0 convert_reduce_fusion
  229.3 4.8 fusion.17
  244.9 4.2 fusion.36
  264.1 6.3 convolution_convert_fusion
  281.6 5.5 all-to-all-done.2
  292.4 11.1 %all-to-all-done.4 = f32[1,256,768]{2,0,1:T(1,128)S(1)} async-done(((f32[1,256,768]{2,0,1:T(1,128)}), f32[1,256,768]{2,0,1:T(1,128)S(1)}, u32[]{:S(2)}, u32[]{:S(2)}) %all-to-all-start.4) | async-done | bytes 786464 | tf_op jit(solution)/shard_map/all_to_all | solution.py:200
  304.4 42.0 %reduce-scatter.7.cloned.1.call-done = bf16[24,768]{1,0:T(8,128)(2,1)} async-done(((bf16[768,768]{1,0:T(8,128)(2,1)}), bf16[24,768]{1,0:T(8,128)(2,1)}) %reduce-scatter.7.cloned.1.call-update) | async-done | bytes 36880 | tf_op jit(solution)/shard_map/reduce_scatter | solution.py:42
  347.7 55.6 %all-gather.16.cloned.1.call-done = f32[32,1,10752]{2,1,0:T(1,128)} async-done(((f32[1,1,10752]{2,1,0:T(1,128)}), f32[32,1,10752]{2,1,0:T(1,128)}) %all-gather.16.cloned.1.call-update) | async-done | bytes 1376272 | tf_op jit(solution)/shard_map/all_gather | solution.py:214
  405.7 4.6 all-to-all-start.5
  418.6 92.5 %reduce-scatter.5.cloned.1.call-done = bf16[24,2304]{1,0:T(8,128)(2,1)} async-done(((bf16[768,2304]{1,0:T(8,128)(2,1)}), bf16[24,2304]{1,0:T(8,128)(2,1)}) %reduce-scatter.5.cloned.1.call-update) | async-done | bytes 110608 | tf_op jit(solution)/shard_map/reduce_scatter | solution.py:42
  512.7 110.3 %reduce-scatter.9.cloned.1.call-done = bf16[24,3072]{1,0:T(8,128)(2,1)} async-done(((bf16[768,3072]{1,0:T(8,128)(2,1)}), bf16[24,3072]{1,0:T(8,128)(2,1)}) %reduce-scatter.9.cloned.1.call-update) | async-done | bytes 147472 | tf_op jit(solution)/shard_map/reduce_scatter | solution.py:42
  624.6 110.7 %reduce-scatter.11.cloned.1.call-done = bf16[96,768]{1,0:T(8,128)(2,1)} async-done(((bf16[3072,768]{1,0:T(8,128)(2,1)}), bf16[96,768]{1,0:T(8,128)(2,1)}) %reduce-scatter.11.cloned.1.call-update) | async-done | bytes 147472 | tf_op jit(solution)/shard_map/reduce_scatter | solution.py:42
  (171 shorter events, 87.1 us)
Async XLA Ops:
  7.2 35.0 %copy-start = (bf16[48,4608]{1,0:T(8,128)(2,1)S(1)}, bf16[48,4608]{1,0:T(8,128)(2,1)}, u32[]{:S(2)}) copy-start(bf16[48,4608]{1,0:T(8,128)(2,1)} %param.17) | copy-start | bytes 1327108
  7.2 66.2 %all-gather.8.cloned.1.call-start = ((), (), s32[]{:S(2)}) async-start(), calls=%async_computation.10 | async-start | bytes 3760128 | tf_op jit(solution)/shard_map/all_gather | solution.py:112
  7.9 96.7 %all-gather.10.cloned.1.call-start = ((), (), s32[]{:S(2)}) async-start(), calls=%async_computation.11 | async-start | bytes 1253376 | tf_op jit(solution)/shard_map/all_gather | solution.py:113
  8.7 150.3 %all-gather.14.cloned.1.call-start = ((), (), s32[]{:S(2)}) async-start(), calls=%async_computation.13 | async-start | bytes 5013504 | tf_op jit(solution)/shard_map/all_gather | solution.py:115
  9.4 203.4 %all-gather.12.cloned.1.call-start = ((), (), s32[]{:S(2)}) async-start(), calls=%async_computation.12 | async-start | bytes 5013504 | tf_op jit(solution)/shard_map/all_gather | solution.py:114
  10.0 33.7 %all-to-all-start = ((bf16[2,128,768]{2,1,0:T(8,128)(2,1)}), bf16[2,128,768]{2,1,0:T(8,128)(2,1)S(1)}, u32[]{:S(2)}, u32[]{:S(2)}) async-start(bf16[2,128,768]{2,1,0:T(8,128)(2,1)} %param.14), calls=%async_computation | async-start | bytes 786432 | tf_op jit(solution)/shard_map/all_to_all | solution.py:91
  43.7 17.9 %all-to-all-start.1 = ((f32[16,1,4608]{2,1,0:T(1,128)}), f32[16,1,4608]{2,1,0:T(1,128)S(1)}, u32[]{:S(2)}, u32[]{:S(2)}) async-start(f32[16,1,4608]{2,1,0:T(1,128)} %copy.61), calls=%async_computation.1 | async-start | bytes 589824 | tf_op jit(solution)/shard_map/all_to_all | solution.py:101
  61.7 10.5 %all-to-all-start.3 = ((bf16[2,128,768]{2,1,0:T(8,128)(2,1)}), bf16[2,128,768]{2,1,0:T(8,128)(2,1)S(1)}, u32[]{:S(2)}, u32[]{:S(2)}) async-start(bf16[2,128,768]{2,1,0:T(8,128)(2,1)} %param.16), calls=%async_computation.3 | async-start | bytes 786432 | tf_op jit(solution)/shard_map/all_to_all | solution.py:92
  65.5 280.9 %reduce-scatter.7.cloned.1.call-start = ((), (), s32[]{:S(2)}) async-start(), calls=%async_computation.15 | async-start | bytes 1216512 | tf_op jit(solution)/shard_map/reduce_scatter | solution.py:42
  212.8 7.1 copy-start.15
  219.9 4.0 copy-start.3
  223.9 3.9 copy-start.4
  229.3 4.8 copy-start.12
  239.5 2.5 copy-start.9
  250.7 152.7 %all-gather.16.cloned.1.call-start = ((), (), s32[]{:S(2)}) async-start(), calls=%async_computation.18 | async-start | bytes 1419264 | tf_op jit(solution)/shard_map/all_gather | solution.py:214
  250.7 3.1 copy-start.2
  254.8 256.3 %reduce-scatter.5.cloned.1.call-start = ((), (), s32[]{:S(2)}) async-start(), calls=%async_computation.14 | async-start | bytes 3649536 | tf_op jit(solution)/shard_map/reduce_scatter | solution.py:42
  258.1 364.9 %reduce-scatter.9.cloned.1.call-start = ((), (), s32[]{:S(2)}) async-start(), calls=%async_computation.16 | async-start | bytes 4866048 | tf_op jit(solution)/shard_map/reduce_scatter | solution.py:42
  263.2 472.2 %reduce-scatter.11.cloned.1.call-start = ((), (), s32[]{:S(2)}) async-start(), calls=%async_computation.17 | async-start | bytes 4866048 | tf_op jit(solution)/shard_map/reduce_scatter | solution.py:42
  270.5 9.4 %copy-start.5 = (f32[256,768]{1,0:T(8,128)S(1)}, f32[256,768]{1,0:T(8,128)}, u32[]{:S(2)}) copy-start(f32[256,768]{1,0:T(8,128)} %get-tuple-element.43) | copy-start | bytes 2359300
  276.5 10.7 %all-to-all-start.2 = ((bf16[2,2,49152]{2,1,0:T(2,128)(2,1)}), bf16[2,2,49152]{2,1,0:T(2,128)(2,1)S(1)}, u32[]{:S(2)}, u32[]{:S(2)}) async-start(bf16[2,2,49152]{2,1,0:T(2,128)(2,1)} %reshape.788), calls=%async_computation.2 | async-start | bytes 786432 | tf_op jit(solution)/shard_map/all_to_all | solution.py:148
  287.2 16.3 %all-to-all-start.4 = ((f32[1,256,768]{2,0,1:T(1,128)}), f32[1,256,768]{2,0,1:T(1,128)S(1)}, u32[]{:S(2)}, u32[]{:S(2)}) async-start(f32[1,256,768]{2,0,1:T(1,128)} %copy.70), calls=%async_computation.4 | async-start | bytes 1572864 | tf_op jit(solution)/shard_map/all_to_all | solution.py:200
  347.7 70.2 %copy-start.14 = (bf16[2,768]{1,0:T(2,128)(2,1)S(1)}, bf16[2,768]{1,0:T(2,128)(2,1)}, u32[]{:S(2)}) copy-start(bf16[2,768]{1,0:T(2,128)(2,1)} %param.15) | copy-start | bytes 9220
  405.7 11.0 %all-to-all-start.5 = ((f32[16,1,96]{2,1,0:T(1,128)}), f32[16,1,96]{2,1,0:T(1,128)S(1)}, u32[]{:S(2)}, u32[]{:S(2)}) async-start(f32[16,1,96]{2,1,0:T(1,128)} %bitcast.31), calls=%async_computation.5 | async-start | bytes 16384 | tf_op jit(solution)/shard_map/all_to_all | solution.py:238
  (8 other events, 12.8 us)
Sparse Core Ops, SparseCore 0:
  10.3 55.0 all-gather.7
  67.7 36.8 all-gather.9
  106.9 51.9 all-gather.13
  161.1 51.6 all-gather.11
  250.8 95.5 reduce-scatter.6
  349.6 53.6 all-gather.15
  408.7 102.3 reduce-scatter.4
  516.6 106.3 reduce-scatter.8
  628.5 106.8 reduce-scatter.10
where the time goes:
time: 745 us; the launch traced here: 744 us
  waiting for transfers between devices  570 us (77%)
  matrix products  60.4 us (8%)
  local copies, waits for them, and re-layouts  29.6 us (4%)
  starting transfers between devices  23.8 us (3%)
  other arithmetic  23 us (3%)
  blocking collectives  22.7 us (3%)
  between operations  14.4 us (2%)
    reduce_scatter x4, waiting for transfers between devices, reduce_rows(): lax.psum_scatter(grad.astype(jnp.bfloat16), ('fsdp', 'sp'), scatter_dimen...  355 us
    all_gather x1, waiting for transfers between devices, body(): lax.all_gather(jnp.concatenate(grad_small), ('fsdp', 'sp'), axis=0)  55.6 us
    all_gather x1, waiting for transfers between devices, body(): down_full = lax.all_gather(w_down, 'fsdp', axis=0, tiled=True)  51.3 us
    all_gather x1, waiting for transfers between devices, body(): up_full = lax.all_gather(w_up, 'fsdp', axis=0, tiled=True)  48.3 us
    all_gather x1, blocking collectives, body(): lax.all_gather(jnp.concatenate(small).reshape(1, padded // 128, 128), 'fs...  22.7 us
    all_gather x1, waiting for transfers between devices, body(): out_full = lax.all_gather(w_out, 'fsdp', axis=0, tiled=True)  18.5 us
  transfers between devices with their start and end apart: 15, of which 13 were waited for; matrix products, arithmetic and copies ran while one was open for 9% of the time, Pallas kernels for 0%

commit v1 on v0

--- a/solution.py
+++ b/solution.py
@@ -7,6 +7,12 @@
 H = 12
 HD = 64
 eps = 1e-06
+
+
+def joined_along(pieces, dim):
+    pieces = jnp.moveaxis(pieces, 0, dim)
+    lengths = pieces.shape
+    return pieces.reshape(*lengths[:dim], lengths[dim] * lengths[dim + 1], *lengths[dim + 2 :])
 
 
 def normalize(values):
@@ -112,7 +118,14 @@
     qkv_full = lax.all_gather(w_qkv, "fsdp", axis=0, tiled=True)
     out_full = lax.all_gather(w_out, "fsdp", axis=0, tiled=True)
     up_full = lax.all_gather(w_up, "fsdp", axis=0, tiled=True)
-    down_full = lax.all_gather(w_down, "fsdp", axis=0, tiled=True)
+    size = lax.axis_size("fsdp")
+    upward = [(i, (i + 1) % size) for i in range(size)]
+    blocks = [w_down]
+    while len(blocks) < size:
+        blocks.append(lax.ppermute(blocks[-1], "fsdp", upward))
+    mine = lax.axis_index("fsdp")
+    blocks = jnp.stack(blocks)[(mine - jnp.arange(size)) % size]
+    down_full = joined_along(blocks, 0)
     normed_one, inverse_one = normalize(inputs)
     attn_in = (normed_one * (1.0 + scale_one) + shift_one).astype(bf16)
     qkv_bias = jnp.concatenate([query_bias, jnp.zeros_like(query_bias), value_bias]).astype(f32)

time: 745 us -> 752 us (level)
  local copies, waits for them, and re-layouts: 29.6 us -> 47.4 us
  waiting for transfers between devices: 570 us -> 557 us
    ppermute x0 -> x15, waiting for transfers between devices: none -> 127 us  [body(): blocks.append(lax.ppermute(blocks[-1], 'fsdp', upward))]
    all_gather x1 -> x0, waiting for transfers between devices: 51.3 us -> none  [body(): down_full = lax.all_gather(w_down, 'fsdp', axis=0, tiled=True)]
    all_gather x1, waiting for transfers between devices: 48.3 us -> 0.02 us  [body(): up_full = lax.all_gather(w_up, 'fsdp', axis=0, tiled=True)]
    all_gather x1, waiting for transfers between devices: 18.5 us -> 0.01 us  [body(): out_full = lax.all_gather(w_out, 'fsdp', axis=0, tiled=True)]
    all_to_all x1, waiting for transfers between devices: 13.6 us -> 0.01 us  [body(): lax.all_to_all(mod_part.reshape(fsdp_count, own_latents * 6 * D), 'fsdp',...]
    unnamed x52 -> x81, local copies, waits for them, and re-layouts: 12.9 us -> 23.6 us
  transfers between devices with their start and end apart: 15 -> 29, of which waited for: 13 -> 22; matrix products, arithmetic and copies ran while one was open for 9% -> 11% of each run, Pallas kernels for 0% -> 0%
where the time goes in v1:
time: 752 us; the launch traced here: 751 us
  waiting for transfers between devices  557 us (74%)
  matrix products  59.8 us (8%)
  local copies, waits for them, and re-layouts  47.4 us (6%)
  starting transfers between devices  26.1 us (3%)
  other arithmetic  23 us (3%)
  blocking collectives  22.8 us (3%)
  between operations  14.9 us (2%)
    reduce_scatter x4, waiting for transfers between devices, reduce_rows(): lax.psum_scatter(grad.astype(jnp.bfloat16), ('fsdp', 'sp'), scatter_dimen...  356 us
    ppermute x15, waiting for transfers between devices, body(): blocks.append(lax.ppermute(blocks[-1], 'fsdp', upward))  127 us
    all_gather x1, waiting for transfers between devices, body(): lax.all_gather(jnp.concatenate(grad_small), ('fsdp', 'sp'), axis=0)  55.6 us
    unnamed x81, local copies, waits for them, and re-layouts  23.6 us
    all_gather x1, blocking collectives, body(): lax.all_gather(jnp.concatenate(small).reshape(1, padded // 128, 128), 'fs...  22.8 us
  transfers between devices with their start and end apart: 29, of which 22 were waited for; matrix products, arithmetic and copies ran while one was open for 11% of the time, Pallas kernels for 0%

profile of v1, /device:TPU:0, one launch (start us, length us, event | category | flops | bytes accessed | tf_op | source)
XLA Modules:
  0.0 751.1 jit_solution(12506185615900682669)
XLA Ops:
  18.5 22.8 %all_gather.18 = bf16[16,32,128]{2,1,0:T(8,128)(2,1)S(1)} all-gather(bf16[1,32,128]{2,1,0:T(8,128)(2,1)S(1)} %bitcast.226), channel_id=1, replica_groups=mesh['fsdp'=16,'sp'=2] {'fsdp'}, dimensions={0}, use_global_device_ids=true | all-gather | bytes 139264 | tf_op jit(solution)/shard_map/all_gather | solution.py:86
  42.2 13.9 %collective-permute-done.1 = bf16[192,768]{1,0:T(8,128)(2,1)S(1)} collective-permute-done((bf16[192,768]{1,0:T(8,128)(2,1)S(1)}, bf16[192,768]{1,0:T(8,128)(2,1)S(1)}, u32[]{:S(2)}, u32[]{:S(2)}) %collective-permute-start.1) | collective-permute-done | bytes 294944 | tf_op jit(solution)/shard_map/ppermute | solution.py:125
  56.2 10.4 %collective-permute-done.2 = bf16[192,768]{1,0:T(8,128)(2,1)S(1)} collective-permute-done((bf16[192,768]{1,0:T(8,128)(2,1)S(1)}, bf16[192,768]{1,0:T(8,128)(2,1)S(1)}, u32[]{:S(2)}, u32[]{:S(2)}) %collective-permute-start.2) | collective-permute-done | bytes 294944 | tf_op jit(solution)/shard_map/ppermute | solution.py:125
  67.4 8.1 %collective-permute-done.3 = bf16[192,768]{1,0:T(8,128)(2,1)S(1)} collective-permute-done((bf16[192,768]{1,0:T(8,128)(2,1)S(1)}, bf16[192,768]{1,0:T(8,128)(2,1)S(1)}, u32[]{:S(2)}, u32[]{:S(2)}) %collective-permute-start.3) | collective-permute-done | bytes 294944 | tf_op jit(solution)/shard_map/ppermute | solution.py:125
  77.1 5.8 all-to-all-start.1
  85.8 11.0 %collective-permute-done.5 = bf16[192,768]{1,0:T(8,128)(2,1)} collective-permute-done((bf16[192,768]{1,0:T(8,128)(2,1)S(1)}, bf16[192,768]{1,0:T(8,128)(2,1)}, u32[]{:S(2)}, u32[]{:S(2)}) %collective-permute-start.5) | collective-permute-done | bytes 294944 | tf_op jit(solution)/shard_map/ppermute | solution.py:125
  101.3 5.9 collective-permute-done.6
  108.4 8.0 %collective-permute-done.7 = bf16[192,768]{1,0:T(8,128)(2,1)} collective-permute-done((bf16[192,768]{1,0:T(8,128)(2,1)}, bf16[192,768]{1,0:T(8,128)(2,1)}, u32[]{:S(2)}, u32[]{:S(2)}) %collective-permute-start.7) | collective-permute-done | bytes 294944 | tf_op jit(solution)/shard_map/ppermute | solution.py:125
  117.4 14.2 %collective-permute-done.8 = bf16[192,768]{1,0:T(8,128)(2,1)S(1)} collective-permute-done((bf16[192,768]{1,0:T(8,128)(2,1)}, bf16[192,768]{1,0:T(8,128)(2,1)S(1)}, u32[]{:S(2)}, u32[]{:S(2)}) %collective-permute-start.8) | collective-permute-done | bytes 294944 | tf_op jit(solution)/shard_map/ppermute | solution.py:125
  133.0 7.4 collective-permute-done.9
  142.9 12.8 %collective-permute-done.10 = bf16[192,768]{1,0:T(8,128)(2,1)S(1)} collective-permute-done((bf16[192,768]{1,0:T(8,128)(2,1)S(1)}, bf16[192,768]{1,0:T(8,128)(2,1)S(1)}, u32[]{:S(2)}, u32[]{:S(2)}) %collective-permute-start.10) | collective-permute-done | bytes 294944 | tf_op jit(solution)/shard_map/ppermute | solution.py:125
  159.1 11.0 %collective-permute-done.11 = bf16[192,768]{1,0:T(8,128)(2,1)S(1)} collective-permute-done((bf16[192,768]{1,0:T(8,128)(2,1)S(1)}, bf16[192,768]{1,0:T(8,128)(2,1)S(1)}, u32[]{:S(2)}, u32[]{:S(2)}) %collective-permute-start.11) | collective-permute-done | bytes 294944 | tf_op jit(solution)/shard_map/ppermute | solution.py:125
  171.6 7.4 collective-permute-done.12
  180.5 7.3 collective-permute-done.13
  189.3 7.4 collective-permute-done.14
  222.5 6.4 convert_reduce_fusion
  272.6 6.3 convolution_convert_fusion
  290.1 6.2 all-to-all-done.2
  301.5 8.4 %all-to-all-done.4 = f32[1,256,768]{2,0,1:T(1,128)S(1)} async-done(((f32[1,256,768]{2,0,1:T(1,128)}), f32[1,256,768]{2,0,1:T(1,128)S(1)}, u32[]{:S(2)}, u32[]{:S(2)}) %all-to-all-start.4) | async-done | bytes 786464 | tf_op jit(solution)/shard_map/all_to_all | solution.py:213
  310.8 43.0 %reduce-scatter.7.cloned.1.call-done = bf16[24,768]{1,0:T(8,128)(2,1)} async-done(((bf16[768,768]{1,0:T(8,128)(2,1)}), bf16[24,768]{1,0:T(8,128)(2,1)}) %reduce-scatter.7.cloned.1.call-update) | async-done | bytes 36880 | tf_op jit(solution)/shard_map/reduce_scatter | solution.py:48
  355.3 55.6 %all-gather.13.cloned.1.call-done = f32[32,1,10752]{2,1,0:T(1,128)} async-done(((f32[1,1,10752]{2,1,0:T(1,128)}), f32[32,1,10752]{2,1,0:T(1,128)}) %all-gather.13.cloned.1.call-update) | async-done | bytes 1376272 | tf_op jit(solution)/shard_map/all_gather | solution.py:227
  426.2 92.3 %reduce-scatter.5.cloned.1.call-done = bf16[24,2304]{1,0:T(8,128)(2,1)} async-done(((bf16[768,2304]{1,0:T(8,128)(2,1)}), bf16[24,2304]{1,0:T(8,128)(2,1)}) %reduce-scatter.5.cloned.1.call-update) | async-done | bytes 110608 | tf_op jit(solution)/shard_map/reduce_scatter | solution.py:48
  520.1 110.5 %reduce-scatter.9.cloned.1.call-done = bf16[24,3072]{1,0:T(8,128)(2,1)} async-done(((bf16[768,3072]{1,0:T(8,128)(2,1)}), bf16[24,3072]{1,0:T(8,128)(2,1)}) %reduce-scatter.9.cloned.1.call-update) | async-done | bytes 147472 | tf_op jit(solution)/shard_map/reduce_scatter | solution.py:48
  632.2 110.3 %reduce-scatter.11.cloned.1.call-done = bf16[96,768]{1,0:T(8,128)(2,1)} async-done(((bf16[3072,768]{1,0:T(8,128)(2,1)}), bf16[96,768]{1,0:T(8,128)(2,1)}) %reduce-scatter.11.cloned.1.call-update) | async-done | bytes 147472 | tf_op jit(solution)/shard_map/reduce_scatter | solution.py:48
  (232 shorter events, 143.7 us)
Async XLA Ops:
  7.2 195.5 %all-gather.7.cloned.1.call-start = ((), (), s32[]{:S(2)}) async-start(), calls=%async_computation.10 | async-start | bytes 3760128 | tf_op jit(solution)/shard_map/all_gather | solution.py:118
  7.9 207.5 %all-gather.9.cloned.1.call-start = ((), (), s32[]{:S(2)}) async-start(), calls=%async_computation.11 | async-start | bytes 1253376 | tf_op jit(solution)/shard_map/all_gather | solution.py:119
  8.7 68.4 %all-to-all-start = ((bf16[2,128,768]{2,1,0:T(8,128)(2,1)}), bf16[2,128,768]{2,1,0:T(8,128)(2,1)S(1)}, u32[]{:S(2)}, u32[]{:S(2)}) async-start(bf16[2,128,768]{2,1,0:T(8,128)(2,1)} %param.14), calls=%async_computation | async-start | bytes 786432 | tf_op jit(solution)/shard_map/all_to_all | solution.py:97
  12.9 205.5 %all-gather.11.cloned.1.call-start = ((), (), s32[]{:S(2)}) async-start(), calls=%async_computation.12 | async-start | bytes 5013504 | tf_op jit(solution)/shard_map/all_gather | solution.py:120
  12.9 28.8 %collective-permute-start = (bf16[192,768]{1,0:T(8,128)(2,1)}, bf16[192,768]{1,0:T(8,128)(2,1)S(1)}, u32[]{:S(2)}, u32[]{:S(2)}) collective-permute-start(bf16[192,768]{1,0:T(8,128)(2,1)} %param.26), channel_id=1, source_target_pairs={{0,2},{2,4},{4,6},{6,8},{8,10},{10,12},{12,14},{14,16},{16,18},{18... | collective-permute-start | bytes 884744 | tf_op jit(solution)/shard_map/ppermute | solution.py:125
  41.7 14.3 %collective-permute-start.1 = (bf16[192,768]{1,0:T(8,128)(2,1)S(1)}, bf16[192,768]{1,0:T(8,128)(2,1)S(1)}, u32[]{:S(2)}, u32[]{:S(2)}) collective-permute-start(bf16[192,768]{1,0:T(8,128)(2,1)S(1)} %collective-permute-done), channel_id=1, source_target_pairs={{0,2},{2,4},{4,6},{6,8},{8,10},{10,12},{12,14},{14,16},{16,18},{18... | collective-permute-start | bytes 884744 | tf_op jit(solution)/shard_map/ppermute | solution.py:125
  56.0 10.6 %collective-permute-start.2 = (bf16[192,768]{1,0:T(8,128)(2,1)S(1)}, bf16[192,768]{1,0:T(8,128)(2,1)S(1)}, u32[]{:S(2)}, u32[]{:S(2)}) collective-permute-start(bf16[192,768]{1,0:T(8,128)(2,1)S(1)} %collective-permute-done.1), channel_id=1, source_target_pairs={{0,2},{2,4},{4,6},{6,8},{8,10},{10,12},{12,14},{14,16},{16,18},{18... | collective-permute-start | bytes 884744 | tf_op jit(solution)/shard_map/ppermute | solution.py:125
  75.5 10.1 %collective-permute-start.4 = (bf16[192,768]{1,0:T(8,128)(2,1)S(1)}, bf16[192,768]{1,0:T(8,128)(2,1)S(1)}, u32[]{:S(2)}, u32[]{:S(2)}) collective-permute-start(bf16[192,768]{1,0:T(8,128)(2,1)S(1)} %collective-permute-done.3), channel_id=1, source_target_pairs={{0,2},{2,4},{4,6},{6,8},{8,10},{10,12},{12,14},{14,16},{16,18},{18... | collective-permute-start | bytes 884744 | tf_op jit(solution)/shard_map/ppermute | solution.py:125
  77.1 19.7 %all-to-all-start.1 = ((f32[16,1,4608]{2,1,0:T(1,128)}), f32[16,1,4608]{2,1,0:T(1,128)S(1)}, u32[]{:S(2)}, u32[]{:S(2)}) async-start(f32[16,1,4608]{2,1,0:T(1,128)} %copy.61), calls=%async_computation.1 | async-start | bytes 589824 | tf_op jit(solution)/shard_map/all_to_all | solution.py:107
  85.6 11.2 %collective-permute-start.5 = (bf16[192,768]{1,0:T(8,128)(2,1)S(1)}, bf16[192,768]{1,0:T(8,128)(2,1)}, u32[]{:S(2)}, u32[]{:S(2)}) collective-permute-start(bf16[192,768]{1,0:T(8,128)(2,1)S(1)} %collective-permute-done.4), channel_id=1, source_target_pairs={{0,2},{2,4},{4,6},{6,8},{8,10},{10,12},{12,14},{14,16},{16,18},{18... | collective-permute-start | bytes 884744 | tf_op jit(solution)/shard_map/ppermute | solution.py:125
  96.8 10.4 %collective-permute-start.6 = (bf16[192,768]{1,0:T(8,128)(2,1)}, bf16[192,768]{1,0:T(8,128)(2,1)}, u32[]{:S(2)}, u32[]{:S(2)}) collective-permute-start(bf16[192,768]{1,0:T(8,128)(2,1)} %collective-permute-done.5), channel_id=1, source_target_pairs={{0,2},{2,4},{4,6},{6,8},{8,10},{10,12},{12,14},{14,16},{16,18},{18... | collective-permute-start | bytes 884744 | tf_op jit(solution)/shard_map/ppermute | solution.py:125
  96.8 10.5 %all-to-all-start.3 = ((bf16[2,128,768]{2,1,0:T(8,128)(2,1)}), bf16[2,128,768]{2,1,0:T(8,128)(2,1)S(1)}, u32[]{:S(2)}, u32[]{:S(2)}) async-start(bf16[2,128,768]{2,1,0:T(8,128)(2,1)} %param.16), calls=%async_computation.3 | async-start | bytes 786432 | tf_op jit(solution)/shard_map/all_to_all | solution.py:98
  100.3 253.6 %reduce-scatter.7.cloned.1.call-start = ((), (), s32[]{:S(2)}) async-start(), calls=%async_computation.14 | async-start | bytes 1216512 | tf_op jit(solution)/shard_map/reduce_scatter | solution.py:48
  107.2 9.2 %collective-permute-start.7 = (bf16[192,768]{1,0:T(8,128)(2,1)}, bf16[192,768]{1,0:T(8,128)(2,1)}, u32[]{:S(2)}, u32[]{:S(2)}) collective-permute-start(bf16[192,768]{1,0:T(8,128)(2,1)} %collective-permute-done.6), channel_id=1, source_target_pairs={{0,2},{2,4},{4,6},{6,8},{8,10},{10,12},{12,14},{14,16},{16,18},{18... | collective-permute-start | bytes 884744 | tf_op jit(solution)/shard_map/ppermute | solution.py:125
  116.4 15.2 %collective-permute-start.8 = (bf16[192,768]{1,0:T(8,128)(2,1)}, bf16[192,768]{1,0:T(8,128)(2,1)S(1)}, u32[]{:S(2)}, u32[]{:S(2)}) collective-permute-start(bf16[192,768]{1,0:T(8,128)(2,1)} %collective-permute-done.7), channel_id=1, source_target_pairs={{0,2},{2,4},{4,6},{6,8},{8,10},{10,12},{12,14},{14,16},{16,18},{18... | collective-permute-start | bytes 884744 | tf_op jit(solution)/shard_map/ppermute | solution.py:125
  140.4 15.3 %collective-permute-start.10 = (bf16[192,768]{1,0:T(8,128)(2,1)S(1)}, bf16[192,768]{1,0:T(8,128)(2,1)S(1)}, u32[]{:S(2)}, u32[]{:S(2)}) collective-permute-start(bf16[192,768]{1,0:T(8,128)(2,1)S(1)} %collective-permute-done.9), channel_id=1, source_target_pairs={{0,2},{2,4},{4,6},{6,8},{8,10},{10,12},{12,14},{14,16},{16,18},{18... | collective-permute-start | bytes 884744 | tf_op jit(solution)/shard_map/ppermute | solution.py:125
  155.7 14.4 %collective-permute-start.11 = (bf16[192,768]{1,0:T(8,128)(2,1)S(1)}, bf16[192,768]{1,0:T(8,128)(2,1)S(1)}, u32[]{:S(2)}, u32[]{:S(2)}) collective-permute-start(bf16[192,768]{1,0:T(8,128)(2,1)S(1)} %collective-permute-done.10), channel_id=1, source_target_pairs={{0,2},{2,4},{4,6},{6,8},{8,10},{10,12},{12,14},{14,16},{16,18},{18... | collective-permute-start | bytes 884744 | tf_op jit(solution)/shard_map/ppermute | solution.py:125
  259.4 151.5 %all-gather.13.cloned.1.call-start = ((), (), s32[]{:S(2)}) async-start(), calls=%async_computation.17 | async-start | bytes 1419264 | tf_op jit(solution)/shard_map/all_gather | solution.py:227
  263.6 255.0 %reduce-scatter.5.cloned.1.call-start = ((), (), s32[]{:S(2)}) async-start(), calls=%async_computation.13 | async-start | bytes 3649536 | tf_op jit(solution)/shard_map/reduce_scatter | solution.py:48
  266.5 364.0 %reduce-scatter.9.cloned.1.call-start = ((), (), s32[]{:S(2)}) async-start(), calls=%async_computation.15 | async-start | bytes 4866048 | tf_op jit(solution)/shard_map/reduce_scatter | solution.py:48
  271.6 470.9 %reduce-scatter.11.cloned.1.call-start = ((), (), s32[]{:S(2)}) async-start(), calls=%async_computation.16 | async-start | bytes 4866048 | tf_op jit(solution)/shard_map/reduce_scatter | solution.py:48
  284.9 11.4 %all-to-all-start.2 = ((bf16[2,2,49152]{2,1,0:T(2,128)(2,1)}), bf16[2,2,49152]{2,1,0:T(2,128)(2,1)S(1)}, u32[]{:S(2)}, u32[]{:S(2)}) async-start(bf16[2,2,49152]{2,1,0:T(2,128)(2,1)} %reshape.854), calls=%async_computation.2 | async-start | bytes 786432 | tf_op jit(solution)/shard_map/all_to_all | solution.py:161
  296.3 13.6 %all-to-all-start.4 = ((f32[1,256,768]{2,0,1:T(1,128)}), f32[1,256,768]{2,0,1:T(1,128)S(1)}, u32[]{:S(2)}, u32[]{:S(2)}) async-start(f32[1,256,768]{2,0,1:T(1,128)} %copy.70), calls=%async_computation.4 | async-start | bytes 1572864 | tf_op jit(solution)/shard_map/all_to_all | solution.py:213
  413.2 11.0 %all-to-all-start.5 = ((f32[16,1,96]{2,1,0:T(1,128)}), f32[16,1,96]{2,1,0:T(1,128)S(1)}, u32[]{:S(2)}, u32[]{:S(2)}) async-start(f32[16,1,96]{2,1,0:T(1,128)} %bitcast.50), calls=%async_computation.5 | async-start | bytes 16384 | tf_op jit(solution)/shard_map/all_to_all | solution.py:251
  (29 other events, 412.0 us)
Sparse Core Ops, SparseCore 0:
  10.3 52.3 all-gather.6
  65.0 42.3 all-gather.8
  109.7 57.5 all-gather.10
  259.5 94.3 reduce-scatter.6
  357.2 53.6 all-gather.12
  416.1 102.3 reduce-scatter.4
  524.0 106.5 reduce-scatter.8
  636.1 106.4 reduce-scatter.10
